TPU v7x, 512 devices: a whole 4x8x8 slice. The times are simulated.
512 devices in a mesh: lon: 64 (over z_hi, x, y), ch: 8 (over z_lo, core).
Axes of the slice: x: 4, y: 8, z: 8 (z_hi: 2, z_lo: 4; z = z_hi * 4 + z_lo), core: 2. Of those that a mesh axis runs over, the one named last changes fastest.
Arguments:
- coarse: bfloat16 [16, 4, 256, 1024], P(None, None, 'lon', 'ch'), may hold values from -6 to 6
- up_kernel: bfloat16 [4, 4, 1024, 512], P(None, None, 'ch', 'lon'), may hold values from -0.09375 to 0.09375
- up_bias: float32 [512], replicated, may hold values from -3 to 3
- conv_kernel: bfloat16 [3, 3, 512, 512], P(None, None, 'lon'), may hold values from -0.09375 to 0.09375
- conv_bias: float32 [512], replicated, may hold values from -3 to 3
Outputs:
- fine_out: bfloat16 [32, 4, 512, 512], P('ch', None, 'lon')
All inputs are finite; a program needn't handle non-finite values.
Results may differ from a plain program's by a relative error of at most 0.015.
Values may be sent and summed in bfloat16 or wider, within the bound.
A program may use at most 64 MiB of HBM per device.

v0:
```python
import jax
import jax.numpy as jnp
from jax import lax
from jax.sharding import PartitionSpec as P

TAPS = (((1, 1), (3, 0)), ((2, 1), (0, 2)))


def padded_2(block, sides, width, periodic):
    for axis, dim in sides:
        count = lax.axis_size(axis)
        forward = [(i, i + 1) for i in range(count - 1)]
        if periodic:
            forward.append((count - 1, 0))
        backward = [(target, source) for source, target in forward]
        low = lax.ppermute(
            lax.slice_in_dim(block, block.shape[dim] - width, None, axis=dim), axis, forward
        )
        high = lax.ppermute(lax.slice_in_dim(block, 0, width, axis=dim), axis, backward)
        block = jnp.concatenate([low, block, high], axis=dim)
    return block


def tap_dot(piece, weight):
    return jnp.einsum("rbjc,cn->rbjn", piece, weight, preferred_element_type=jnp.float32)


def upsample(padded, lon_count, weights):
    rows = padded.shape[0] - 2
    batch = padded.shape[1]
    phases = []
    for p in range(2):
        columns = []
        for q in range(2):
            total = None
            for a, row_off in TAPS[p]:
                for c, col_off in TAPS[q]:
                    piece = padded[row_off : row_off + rows, :, col_off : col_off + lon_count, :]
                    term = tap_dot(piece, weights[a, c])
                    total = term if total is None else total + term
            columns.append(total)
        phases.append(jnp.stack(columns, axis=3))
    stacked = jnp.stack(phases, axis=1)
    return stacked.reshape(2 * rows, batch, 2 * lon_count, weights.shape[-1])


def shards(coarse, up_kernel, up_bias, conv_kernel, conv_bias):
    lon_dev = coarse.shape[2]
    row_padded = jnp.pad(coarse, ((1, 1), (0, 0), (0, 0), (0, 0)))
    source = jnp.pad(row_padded, ((0, 0), (0, 0), (2, 2), (0, 0)))
    count = lon_dev + 2
    up_full = lax.all_gather(up_kernel, "lon", axis=3, tiled=True)
    partial_value = upsample(source, count, up_full)
    local_fine = partial_value[:, :, 2 : 2 * lon_dev + 2]
    spill = jnp.concatenate(
        [partial_value[:, :, 1:2], partial_value[:, :, 2 * lon_dev + 2 : 2 * lon_dev + 3]], axis=2
    )
    beside_all = padded_2(spill.astype(jnp.bfloat16), (("lon", 2),), 1, True).astype(spill.dtype)
    local_fine = local_fine.at[:, :, 0].add(beside_all[:, :, 0])
    local_fine = local_fine.at[:, :, -1].add(beside_all[:, :, 3])
    summed = lax.psum_scatter(
        local_fine.astype(jnp.bfloat16), "ch", scatter_dimension=0, tiled=True
    ).astype(jnp.float32)
    hidden = jax.nn.gelu(summed + up_bias, approximate=False).astype(jnp.bfloat16)
    widened = padded_2(hidden, (("lon", 2),), 1, True)
    framed = padded_2(widened, (("ch", 0),), 1, False)
    weights = lax.all_gather(conv_kernel, "lon", axis=2, tiled=True)
    band_rows = hidden.shape[0]
    fine_cols = hidden.shape[2]
    result = jnp.zeros(hidden.shape, jnp.float32) + conv_bias
    for d in range(3):
        for t in range(3):
            result = result + tap_dot(
                framed[d : d + band_rows, :, t : t + fine_cols, :], weights[d, t]
            )
    return result.astype(jnp.bfloat16)


def solution(mesh):
    return jax.shard_map(
        shards,
        mesh=mesh,
        in_specs=(
            P(None, None, "lon", "ch"),
            P(None, None, "ch", "lon"),
            P(),
            P(None, None, "lon", None),
            P(),
        ),
        out_specs=P("ch", None, "lon", None),
        check_vma=False,
    )
```

profile of v0, /device:TPU:1, one launch (start us, length us, event | category | flops | bytes accessed | tf_op | source)
XLA Modules:
  0.0 449.0 jit_solution(3137635655831633041)
XLA Ops:
  6.5 1.4 copy.15
  8.0 0.9 copy.14
  8.9 142.8 %all-gather.3.cloned.1.call-done = bf16[4,4,128,512]{2,1,0,3:T(4,128)(2,1)} async-done(((bf16[4,4,128,8]{2,1,0,3:T(4,128)(2,1)}), bf16[4,4,128,512]{2,1,0,3:T(4,128)(2,1)}) %all-gather.3.cloned.1.call-update) | async-done | bytes 2097168 | tf_op jit(solution)/shard_map/all_gather | solution.py:52
  151.7 8.8 %fusion.77 = (bf16[1,1,128,512]{2,1,0,3:T(2,128)(2,1)S(1)}, bf16[1,1,128,512]{2,1,0,3:T(2,128)(2,1)S(1)}, bf16[1,1,128,512]{2,1,0,3:T(2,128)(2,1)}, bf16[1,1,128...) fusion(bf16[4,4,128,512]{2,1,0,3:T(4,128)(2,1)} %all-gather.3.c, ...), kind=kLoop, calls=%fused_computation.133 | loop fusion | bytes 4194304 | tf_op jit(solution)/shard_map/slice | solution.py:39
  160.5 0.8 copy.69
  163.6 0.8 copy.73
  164.4 1.1 fusion.50
  165.5 1.1 fusion.45
  166.7 1.7 copy.74
  170.0 0.8 copy.61
  170.8 1.1 fusion.60
  171.9 1.7 copy.62
  173.6 0.8 copy.63
  175.2 0.8 copy.65
  176.0 1.1 fusion.55
  177.1 1.7 copy.66
  178.9 1.7 copy.67
  181.4 1.2 convolution_add_fusion.5
  182.6 1.2 convolution_add_fusion.4
  187.2 2.0 copy.32
  189.2 0.9 copy.78
  190.6 2.4 collective-permute-start
  193.0 11.2 %collective-permute-start.1 = (bf16[32,4,1,512]{3,2,1,0:T(2,128)(2,1)S(1)}, bf16[32,4,1,512]{3,2,1,0:T(2,128)(2,1)S(1)}, u32[]{:S(2)}, u32[]{:S(2)}) collective-permute-start(bf16[32,4,1,512]{3,2,1,0:T(2,128)(2,1)S(1)} %get-tuple-element.30), channel_id=1, source_target_pairs={{8,0},{16,8},{24,16},{32,24},{40,32},{48,40},{56,48},{64,56},{72,6... | collective-permute-start | bytes 393224 | tf_op jit(solution)/shard_map/ppermute | solution.py:19
  204.2 1.3 copy.33
  206.0 2.0 collective-permute-done
  208.1 1.4 convert_add_fusion
  209.4 2.1 scatter-add.6
  211.6 1.4 fusion.23
  212.9 2.1 scatter-add.9
  215.1 1.2 convert_element_type.21
  217.0 43.6 %reduce-scatter.2.cloned.1.call-done = bf16[4,4,8,512]{3,2,1,0:T(8,128)(2,1)} async-done(((bf16[32,4,8,512]{3,2,1,0:T(8,128)(2,1)}), bf16[4,4,8,512]{3,2,1,0:T(8,128)(2,1)}) %reduce-scatter.2.cloned.1.call-update) | async-done | bytes 131088 | tf_op jit(solution)/shard_map/reduce_scatter | solution.py:61
  260.6 1.5 fusion.21
  262.2 2.3 collective-permute-start.2
  264.5 11.1 %collective-permute-start.3 = (bf16[4,4,1,512]{3,2,1,0:T(2,128)(2,1)S(1)}, bf16[4,4,1,512]{3,2,1,0:T(2,128)(2,1)S(1)}, u32[]{:S(2)}, u32[]{:S(2)}) collective-permute-start(bf16[4,4,1,512]{3,2,1,0:T(2,128)(2,1)S(1)} %get-tuple-element.52), channel_id=1, source_target_pairs={{8,0},{16,8},{24,16},{32,24},{40,32},{48,40},{56,48},{64,56},{72,6... | collective-permute-start | bytes 49160 | tf_op jit(solution)/shard_map/ppermute | solution.py:19
  275.6 1.0 collective-permute-done.3
  276.7 3.7 collective-permute-start.4
  280.4 3.9 collective-permute-start.5
  284.3 2.4 collective-permute-done.5
  287.0 143.2 %all-gather.5.cloned.1.call-done = bf16[3,3,512,512]{3,2,1,0:T(8,128)(2,1)} async-done(((bf16[3,3,8,512]{3,2,1,0:T(8,128)(2,1)}), bf16[3,3,512,512]{3,2,1,0:T(8,128)(2,1)}) %all-gather.5.cloned.1.call-update) | async-done | bytes 4718608 | tf_op jit(solution)/shard_map/all_gather | solution.py:67
  430.2 1.3 fusion.16
  431.5 1.3 fusion.17
  432.8 1.3 fusion.18
  434.1 1.3 fusion.15
  435.3 1.3 fusion.13
  436.6 1.3 fusion.14
  437.9 1.3 fusion.12
  439.2 1.3 fusion.10
  440.5 2.0 fusion.11
  (57 shorter events, 10.8 us)
Async XLA Ops:
  6.5 145.1 %all-gather.3.cloned.1.call-start = ((), (), s32[]{:S(2)}) async-start(), calls=%async_computation.1 | async-start | bytes 2129920 | tf_op jit(solution)/shard_map/all_gather | solution.py:52
  7.9 252.7 %reduce-scatter.2.cloned.1.call-start = ((), (), s32[]{:S(2)}) async-start(), calls=%async_computation.2 | async-start | bytes 1179648 | tf_op jit(solution)/shard_map/reduce_scatter | solution.py:61
  181.4 2.4 copy-start
  181.4 2.7 copy-start.2
  181.4 3.0 copy-start.3
  182.6 2.0 copy-start.1
  183.8 1.1 copy-start.5
  184.1 1.1 copy-start.6
  184.4 1.1 copy-start.4
  184.6 1.1 copy-start.8
  184.9 1.1 copy-start.9
  185.2 1.0 copy-start.7
  190.6 17.4 %collective-permute-start = (bf16[32,4,1,512]{3,2,1,0:T(2,128)(2,1)S(1)}, bf16[32,4,1,512]{3,2,1,0:T(2,128)(2,1)S(1)}, u32[]{:S(2)}, u32[]{:S(2)}) collective-permute-start(bf16[32,4,1,512]{3,2,1,0:T(2,128)(2,1)S(1)} %get-tuple-element.29), channel_id=1, source_target_pairs={{0,8},{8,16},{16,24},{24,32},{32,40},{40,48},{48,56},{56,64},{64,7... | collective-permute-start | bytes 393224 | tf_op jit(solution)/shard_map/ppermute | solution.py:16
  193.0 15.1 %collective-permute-start.1 = (bf16[32,4,1,512]{3,2,1,0:T(2,128)(2,1)S(1)}, bf16[32,4,1,512]{3,2,1,0:T(2,128)(2,1)S(1)}, u32[]{:S(2)}, u32[]{:S(2)}) collective-permute-start(bf16[32,4,1,512]{3,2,1,0:T(2,128)(2,1)S(1)} %get-tuple-element.30), channel_id=1, source_target_pairs={{8,0},{16,8},{24,16},{32,24},{40,32},{48,40},{56,48},{64,56},{72,6... | collective-permute-start | bytes 393224 | tf_op jit(solution)/shard_map/ppermute | solution.py:19
  211.6 49.1 %copy-start.10 = (f32[512]{0:T(512)S(1)}, f32[512]{0:T(512)}, u32[]{:S(2)}) copy-start(f32[512]{0:T(512)} %param.11) | copy-start | bytes 6148
  216.3 214.0 %all-gather.5.cloned.1.call-start = ((), (), s32[]{:S(2)}) async-start(), calls=%async_computation.3 | async-start | bytes 4792320 | tf_op jit(solution)/shard_map/all_gather | solution.py:67
  262.2 13.4 %collective-permute-start.2 = (bf16[4,4,1,512]{3,2,1,0:T(2,128)(2,1)S(1)}, bf16[4,4,1,512]{3,2,1,0:T(2,128)(2,1)S(1)}, u32[]{:S(2)}, u32[]{:S(2)}) collective-permute-start(bf16[4,4,1,512]{3,2,1,0:T(2,128)(2,1)S(1)} %get-tuple-element.51), channel_id=1, source_target_pairs={{0,8},{8,16},{16,24},{24,32},{32,40},{40,48},{48,56},{56,64},{64,7... | collective-permute-start | bytes 49160 | tf_op jit(solution)/shard_map/ppermute | solution.py:16
  264.5 12.1 %collective-permute-start.3 = (bf16[4,4,1,512]{3,2,1,0:T(2,128)(2,1)S(1)}, bf16[4,4,1,512]{3,2,1,0:T(2,128)(2,1)S(1)}, u32[]{:S(2)}, u32[]{:S(2)}) collective-permute-start(bf16[4,4,1,512]{3,2,1,0:T(2,128)(2,1)S(1)} %get-tuple-element.52), channel_id=1, source_target_pairs={{8,0},{16,8},{24,16},{32,24},{40,32},{48,40},{56,48},{64,56},{72,6... | collective-permute-start | bytes 49160 | tf_op jit(solution)/shard_map/ppermute | solution.py:19
  276.7 7.7 %collective-permute-start.4 = (bf16[1,4,10,512]{3,2,1,0:T(8,128)(2,1)S(1)}, bf16[1,4,10,512]{3,2,1,0:T(8,128)(2,1)S(1)}, u32[]{:S(2)}, u32[]{:S(2)}) collective-permute-start(bf16[1,4,10,512]{3,2,1,0:T(8,128)(2,1)S(1)} %get-tuple-element.49), channel_id=1, source_target_pairs={{0,1},{1,2},{2,3},{3,4},{4,5},{5,6},{6,7},{8,9},{9,10},{10,11},{11... | collective-permute-start | bytes 122888 | tf_op jit(solution)/shard_map/ppermute | solution.py:16
  280.4 6.4 %collective-permute-start.5 = (bf16[1,4,10,512]{3,2,1,0:T(8,128)(2,1)S(1)}, bf16[1,4,10,512]{3,2,1,0:T(8,128)(2,1)S(1)}, u32[]{:S(2)}, u32[]{:S(2)}) collective-permute-start(bf16[1,4,10,512]{3,2,1,0:T(8,128)(2,1)S(1)} %get-tuple-element.50), channel_id=1, source_target_pairs={{1,0},{2,1},{3,2},{4,3},{5,4},{6,5},{7,6},{9,8},{10,9},{11,10},{12... | collective-permute-start | bytes 122888 | tf_op jit(solution)/shard_map/ppermute | solution.py:19
  287.0 152.1 %copy-start.11 = (f32[512]{0:T(512)S(1)}, f32[512]{0:T(512)}, u32[]{:S(2)}) copy-start(f32[512]{0:T(512)} %param.13) | copy-start | bytes 6148
Sparse Core Ops, SparseCore 0:
  11.8 139.7 all-gather.2
  216.4 44.2 reduce-scatter.1
  265.0 165.2 all-gather.4
where the time goes:
time: 453 us; the launch traced here: 449 us
  waiting for transfers between devices  336 us (74%)
  local copies, waits for them, and re-layouts  36.9 us (8%)
  starting transfers between devices  34.7 us (8%)
  matrix products  21.6 us (5%)
  between operations  13.6 us (3%)
  other arithmetic  6.35 us (1%)
    all_gather x1, waiting for transfers between devices, shards(): weights = lax.all_gather(conv_kernel, 'lon', axis=2, tiled=True)  143 us
    all_gather x1, waiting for transfers between devices, shards(): up_full = lax.all_gather(up_kernel, 'lon', axis=3, tiled=True)  143 us
    reduce_scatter x1, waiting for transfers between devices, shards(): lax.psum_scatter(local_fine.astype(jnp.bfloat16), 'ch', scatter_dimension...  43.6 us
    ppermute x3, starting transfers between devices, padded_2(): lax.ppermute(lax.slice_in_dim(block, 0, width, axis=dim), axis, backward)  26.3 us
    dot_general x25, matrix products, tap_dot(): jnp.einsum('rbjc,cn->rbjn', piece, weight, preferred_element_type=jnp.flo...  21.6 us
    unnamed x42, local copies, waits for them, and re-layouts  18.6 us
  transfers between devices with their start and end apart: 9, of which 6 were waited for; matrix products, arithmetic and copies ran while one was open for 1% of the time, Pallas kernels for 0%

commit v1 on v0

v1 whole, which is shorter than its diff:
```python
import jax
import jax.numpy as jnp
from jax import lax
from jax.experimental import pallas as pl
from jax.experimental.pallas import tpu as pltpu
from jax.sharding import PartitionSpec as P

MESH = pl.DeviceIdType.MESH
F32, BF16 = jnp.float32, jnp.bfloat16
NX, NY = 4, 8
TAPS = (((1, 1), (3, 0)), ((2, 1), (0, 2)))
PHASES = ((0, 0), (0, 1), (1, 0), (1, 1))
N_SEM = 256


def grid_of(rows, cols):
    return (
        lax.broadcasted_iota(jnp.int32, (rows, cols), 0),
        lax.broadcasted_iota(jnp.int32, (rows, cols), 1),
    )


def pick(mask):
    return jnp.where(mask, 1.0, 0.0).astype(BF16)


def dot(a, b):
    return jnp.dot(a, b, preferred_element_type=F32)


def dot_t(a, b):
    return lax.dot_general(a, b, (((1,), (1,)), ((), ())), preferred_element_type=F32)


def kernel(
    coarse, upk, upb, ck, cb, out,
    uw, cw, ce, nbo, ne, act, part, recv, hid, es, er, g,
    send_sem, recv_sem, local_sem,
):
    lon = lax.axis_index("lon")
    k = lax.axis_index("ch")
    zh, x, y = lon // 32, lax.rem(lon // 8, 4), lax.rem(lon, 8)
    zl, c = k // 2, lax.rem(k, 2)
    other = 1 - zh
    sib = k + 1 - 2 * c
    left, right = lax.rem(lon + 63, 64), lax.rem(lon + 1, 64)

    def dev(xx, yy, plane=None):
        return {"lon": (zh if plane is None else plane) * 32 + xx * 8 + yy, "ch": k}

    def at(l, kk):
        return {"lon": l, "ch": kk}

    def ring(v, d, n):
        return lax.rem(v + (d % n), n)

    sibling = at(lon, sib)

    barrier = pltpu.get_barrier_semaphore()

    def greet(device):
        pl.semaphore_signal(barrier, inc=1, device_id=device, device_id_type=MESH)

    for d in range(1, NX):
        greet(dev(ring(x, d, NX), y))
    for d in range(1, NY):
        greet(dev(x, ring(y, d, NY)))
    greet(dev(x, y, other))
    for d in range(1, 4):
        greet(at(lon, ring(zl, d, 4) * 2 + c))
    for side in (left, right):
        greet(at(side, k))

    @pl.when(k > 0)
    def _():
        for l in (left, lon, right):
            greet(at(l, k - 1))

    @pl.when(k < 7)
    def _():
        for l in (left, lon, right):
            greet(at(l, k + 1))

    pl.semaphore_wait(barrier, 16 + 3 * ((k + 7) // 8) + 3 * ((14 - k) // 8))

    state = {"sem": 0, "local": 0}
    sends = []

    def describe(src, dst, device, index=None):
        if index is None:
            index = state["sem"]
            state["sem"] += 1
        return pltpu.make_async_remote_copy(
            src_ref=src, dst_ref=dst, send_sem=send_sem.at[index], recv_sem=recv_sem.at[index],
            device_id=device, device_id_type=MESH,
        )

    def send(src, dst, device):
        copy = describe(src, dst, device)
        copy.start()
        sends.append(copy)
        return copy

    def local(src, dst):
        copy = pltpu.make_async_copy(src, dst, local_sem.at[state["local"]])
        state["local"] += 1
        copy.start()
        return copy

    class Gather:
        def __init__(self, ref, lanes, source, taps_a, taps_b, start):
            self.ref, self.lanes, self.source = ref, lanes, source
            self.a, self.b, self.t = taps_a, taps_b, start
            self.mirrors = []
            block = self.block(zh, x, y, pl.ds(0, taps_a.size + taps_b.size))
            self.own = local(source, block)
            self.z = send(source, block, dev(x, y, other))
            self.own_done = False

        def block(self, plane, xx, yy, taps):
            return self.ref.at[taps, plane * 4 + xx, pl.ds(pl.multiple_of(yy * 8, 8), 8), self.lanes]

        def by_x(self, plane, xx):
            return self.ref.at[self.b, plane * 4 + xx, :, self.lanes]

        def by_y(self, plane, yy):
            return self.ref.at[
                self.a, pl.ds(plane * 4, 4), pl.ds(pl.multiple_of(yy * 8, 8), 8), self.lanes
            ]

        def mirror(self, unit):
            self.mirrors.append(send(unit, unit, sibling))

        def first(self, plane, far, taps, count, coordinate, device):
            block = self.block(plane, x, y, taps)
            source = block if far else self.source.at[taps]
            return [send(source, block, device(ring(coordinate, d, count))) for d in range(1, count)]

        def settle(self, far):
            if not far and not self.own_done:
                self.own.wait()
                self.own_done = True

        def arrive(self, far):
            if far and self.z is not None:
                self.z.wait_recv()
                self.z = None

        def chain_b(self, far):
            plane = other if far else zh
            t = self.t + (4.2 if far else 0.0)
            if far:
                yield t
                self.arrive(far)
            copies = self.first(plane, far, self.b, NY, y, lambda yy: dev(x, yy))
            yield t + 4.0
            for copy in copies:
                copy.wait_recv()
            self.settle(far)
            unit = self.by_x(plane, x)
            to_right = send(unit, unit, dev(ring(x, 1, NX), y))
            to_left = send(unit, unit, dev(ring(x, -1, NX), y))
            self.mirror(unit)
            yield t + 7.0
            to_right.wait_recv()
            to_left.wait_recv()
            from_left, from_right = self.by_x(plane, ring(x, -1, NX)), self.by_x(plane, ring(x, 1, NX))
            if far:
                forward = send(from_right, from_right, dev(ring(x, -1, NX), y))
            else:
                forward = send(from_left, from_left, dev(ring(x, 1, NX), y))
            self.mirror(from_left)
            self.mirror(from_right)
            yield t + 10.0
            forward.wait_recv()
            self.mirror(self.by_x(plane, ring(x, 2, NX)))

        def chain_a(self, far):
            plane = other if far else zh
            t = self.t + (4.2 if far else 0.0)
            if far:
                yield t
                self.arrive(far)
            copies = self.first(plane, far, self.a, NX, x, lambda xx: dev(xx, y))
            yield t + 2.5
            for copy in copies:
                copy.wait_recv()
            self.settle(far)
            unit = self.by_y(plane, y)
            up = send(unit, unit, dev(x, ring(y, 1, NY)))
            down = send(unit, unit, dev(x, ring(y, -1, NY)))
            self.mirror(unit)
            ups, downs = (3, 4) if far else (4, 3)
            for step in range(1, 5):
                yield t + 2.5 + 2.0 * step
                if step <= ups:
                    up.wait_recv()
                    unit = self.by_y(plane, ring(y, -step, NY))
                    if step < ups:
                        up = send(unit, unit, dev(x, ring(y, 1, NY)))
                    self.mirror(unit)
                if step <= downs:
                    down.wait_recv()
                    unit = self.by_y(plane, ring(y, step, NY))
                    if step < downs:
                        down = send(unit, unit, dev(x, ring(y, -1, NY)))
                    self.mirror(unit)

        def chains(self):
            made = []
            for far in (False, True):
                if self.b.size:
                    made.append(self.chain_b(far))
                if self.a.size:
                    made.append(self.chain_a(far))
            return made

        def finish(self):
            for copy in self.mirrors:
                copy.wait_recv()

    def run(chains):
        waiting = []
        for order, chain in enumerate(chains):
            step = next(chain, None)
            if step is not None:
                waiting.append((step, order, chain))
        while waiting:
            waiting.sort(key=lambda item: item[:2])
            _, order, chain = waiting.pop(0)
            step = next(chain, None)
            if step is not None:
                waiting.append((step, order, chain))

    c128, c256 = pl.multiple_of(c * 128, 128), pl.multiple_of(c * 256, 256)
    up_gather = Gather(uw, pl.ds(c128, 128), upk, pl.ds(0, 6), pl.ds(6, 10), 0.0)
    up_chains = up_gather.chains()
    firsts = [chain for chain in up_chains]

    block = coarse[...].reshape(256, 128)
    m, n = grid_of(64, 256)
    ce[0] = dot(pick(n == 4 * m), block).astype(BF16)
    ce[1] = dot(pick(n == 4 * m + 3), block).astype(BF16)
    arrivals = [send(coarse, nbo, sibling)]

    def beside(kk):
        return [
            send(ce.at[1], ne.at[c, 0], at(right, kk)),
            send(ce.at[0], ne.at[c, 1], at(left, kk)),
        ]

    arrivals += beside(k) + beside(sib)

    def act_chain():
        yield 3.9
        for copy in arrivals:
            copy.wait_recv()
        act[:, pl.ds(0, 1)] = jnp.zeros((3, 1, 16, 256), BF16)
        act[:, pl.ds(17, 1)] = jnp.zeros((3, 1, 16, 256), BF16)
        row, col = grid_of(256, 256)
        low = pick((col == row - 1) & ((row & 3) != 0))
        high = pick((col == row + 1) & ((row & 3) != 3))
        row, col = grid_of(256, 64)
        low_edge, high_edge = pick(row == 4 * col), pick(row == 4 * col + 3)
        for mine in (True, False):
            parity = c if mine else 1 - c
            lanes = pl.ds(pl.multiple_of(parity * 128, 128), 128)
            here = block if mine else nbo[...].reshape(256, 128)
            before = dot(low, here) + dot(low_edge, ne[parity, 0])
            after = dot(high, here) + dot(high_edge, ne[parity, 1])
            act[0, pl.ds(1, 16), :, lanes] = before.astype(BF16).reshape(16, 16, 128)
            act[1, pl.ds(1, 16), :, lanes] = here.reshape(16, 16, 128)
            act[2, pl.ds(1, 16), :, lanes] = after.astype(BF16).reshape(16, 16, 128)

    run(firsts + [act_chain()])
    conv_gather = Gather(cw, pl.ds(c256, 256), ck.at[:, :, pl.ds(c256, 256)], pl.ds(0, 4), pl.ds(4, 5), 20.0)
    conv_chains = conv_gather.chains()
    up_gather.finish()

    scatters = []
    for phase, (p, q) in enumerate(PHASES):
        total = None
        for a, row_off in TAPS[p]:
            for t, col_off in TAPS[q]:
                piece = jnp.concatenate(
                    [act[col_off, pl.ds(4 * band + 2 * c + row_off, 2)].reshape(32, 256) for band in range(4)],
                    axis=0,
                )
                term = dot_t(piece, uw[4 * a + t].reshape(512, 256))
                total = term if total is None else total + term
        part[:, phase] = total.astype(BF16).reshape(4, 2, 16, 512)
        for d in range(1, 4):
            target = ring(zl, d, 4)
            scatters.append(send(part.at[target, phase], recv.at[zl, phase], at(lon, target * 2 + c)))

    def mid_chain():
        yield 26.0
        for phase, (p, q) in enumerate(PHASES):
            total = part[zl, phase].astype(F32)
            for d in range(1, 4):
                scatters[3 * phase + d - 1].wait_recv()
                total = total + recv[ring(zl, -d, 4), phase].astype(F32)
            v = total + upb[...].reshape(1, 1, 512)
            h = (0.5 * v * (1.0 + lax.erf(v * (0.5**0.5)))).astype(BF16)
            hid[q, 1 + p] = h[0]
            hid[q, 3 + p] = h[1]
        m, n = grid_of(32, 64)
        wanted = 4 * (4 * (m >> 3) + (m & 7))
        real = (m & 7) < 4
        es[0] = dot(pick((n == wanted) & real), hid[0, pl.ds(1, 4)].reshape(64, 512)).astype(BF16).reshape(4, 8, 512)
        es[1] = dot(pick((n == wanted + 3) & real), hid[1, pl.ds(1, 4)].reshape(64, 512)).astype(BF16).reshape(4, 8, 512)
        edges = [
            send(es.at[1], er.at[0, pl.ds(1, 4)], at(right, k)),
            send(es.at[0], er.at[1, pl.ds(1, 4)], at(left, k)),
        ]
        first = state["sem"]
        state["sem"] += 6
        upward = lambda: [
            describe(hid.at[:, pl.ds(4, 1)], hid.at[:, pl.ds(0, 1)], at(lon, k + 1), first),
            describe(es.at[1, pl.ds(3, 1)], er.at[0, pl.ds(0, 1)], at(right, k + 1), first + 1),
            describe(es.at[0, pl.ds(3, 1)], er.at[1, pl.ds(0, 1)], at(left, k + 1), first + 2),
        ]
        downward = lambda: [
            describe(hid.at[:, pl.ds(1, 1)], hid.at[:, pl.ds(5, 1)], at(lon, k - 1), first + 3),
            describe(es.at[1, pl.ds(0, 1)], er.at[0, pl.ds(5, 1)], at(right, k - 1), first + 4),
            describe(es.at[0, pl.ds(0, 1)], er.at[1, pl.ds(5, 1)], at(left, k - 1), first + 5),
        ]

        @pl.when(k < 7)
        def _():
            for copy in upward():
                copy.start()

        @pl.when(k > 0)
        def _():
            for copy in downward():
                copy.start()

        yield 30.0
        for copy in edges:
            copy.wait_recv()

        @pl.when(k > 0)
        def _():
            for copy in upward():
                copy.wait_recv()

        @pl.when(k < 7)
        def _():
            for copy in downward():
                copy.wait_recv()

        @pl.when(k < 7)
        def _():
            for copy in upward():
                copy.wait_send()

        @pl.when(k > 0)
        def _():
            for copy in downward():
                copy.wait_send()

        @pl.when(k == 0)
        def _():
            hid[:, pl.ds(0, 1)] = jnp.zeros((2, 1, 16, 512), BF16)
            er[:, pl.ds(0, 1)] = jnp.zeros((2, 1, 8, 512), BF16)

        @pl.when(k == 7)
        def _():
            hid[:, pl.ds(5, 1)] = jnp.zeros((2, 1, 16, 512), BF16)
            er[:, pl.ds(5, 1)] = jnp.zeros((2, 1, 8, 512), BF16)

        even, odd = hid[0].reshape(96, 512), hid[1].reshape(96, 512)
        row, col = grid_of(96, 96)
        low = pick((col == row - 1) & ((row & 3) != 0))
        high = pick((col == row + 1) & ((row & 3) != 3))
        row, col = grid_of(96, 48)
        place = 8 * (row >> 4) + ((row >> 2) & 3)
        low_edge = pick((col == place) & ((row & 3) == 0))
        high_edge = pick((col == place) & ((row & 3) == 3))
        before = dot(low, odd) + dot(low_edge, er[0].reshape(48, 512))
        after = dot(high, even) + dot(high_edge, er[1].reshape(48, 512))
        g[0, :, 0] = before.astype(BF16).reshape(6, 16, 512)
        g[0, :, 1] = hid[0]
        g[1, :, 0] = hid[0]
        g[1, :, 1] = hid[1]
        g[2, :, 0] = hid[1]
        g[2, :, 1] = after.astype(BF16).reshape(6, 16, 512)

    run(conv_chains + [mid_chain()])
    conv_gather.finish()

    total = None
    for d in range(3):
        for t in range(3):
            term = dot(g[t, pl.ds(d, 4)].reshape(128, 512), cw[3 * d + t].reshape(512, 512))
            total = term if total is None else total + term
    total = total + cb[...]
    out[...] = total.astype(BF16).reshape(4, 2, 16, 512)
    for copy in sends:
        copy.wait_send()


def shards(coarse, up_kernel, up_bias, conv_kernel, conv_bias):
    vmem = pl.BlockSpec(memory_space=pltpu.VMEM)
    result = pl.pallas_call(
        kernel,
        out_shape=jax.ShapeDtypeStruct((4, 2, 16, 512), BF16),
        in_specs=[vmem] * 5,
        out_specs=vmem,
        scratch_shapes=[
            pltpu.VMEM((16, 8, 64, 256), BF16),
            pltpu.VMEM((9, 8, 64, 512), BF16),
            pltpu.VMEM((2, 64, 128), BF16),
            pltpu.VMEM((16, 16, 128), BF16),
            pltpu.VMEM((2, 2, 64, 128), BF16),
            pltpu.VMEM((3, 18, 16, 256), BF16),
            pltpu.VMEM((4, 4, 2, 16, 512), BF16),
            pltpu.VMEM((4, 4, 2, 16, 512), BF16),
            pltpu.VMEM((2, 6, 16, 512), BF16),
            pltpu.VMEM((2, 4, 8, 512), BF16),
            pltpu.VMEM((2, 6, 8, 512), BF16),
            pltpu.VMEM((3, 6, 2, 16, 512), BF16),
            pltpu.SemaphoreType.DMA((N_SEM,)),
            pltpu.SemaphoreType.DMA((N_SEM,)),
            pltpu.SemaphoreType.DMA((2,)),
        ],
        compiler_params=pltpu.CompilerParams(collective_id=0, has_side_effects=True),
    )(
        coarse.reshape(16, 16, 128),
        up_kernel.transpose(0, 1, 3, 2).reshape(16, 8, 128),
        up_bias.reshape(1, 512),
        conv_kernel.reshape(9, 8, 512),
        conv_bias.reshape(1, 512),
    )
    return result.reshape(4, 2, 4, 4, 512).transpose(0, 2, 3, 1, 4).reshape(4, 4, 8, 512)


def solution(mesh):
    return jax.shard_map(
        shards,
        mesh=mesh,
        in_specs=(
            P(None, None, "lon", "ch"),
            P(None, None, "ch", "lon"),
            P(),
            P(None, None, "lon", None),
            P(),
        ),
        out_specs=P("ch", None, "lon", None),
        check_vma=False,
    )
```

time: 453 us -> 86.2 us (0.19)
  waiting for transfers between devices: 336 us -> 0 us
  Pallas kernels: 0 us -> 84.2 us
  local copies, waits for them, and re-layouts: 36.9 us -> 1.79 us
  starting transfers between devices: 34.7 us -> 0 us
  matrix products: 21.6 us -> 0 us
  between operations: 13.6 us -> 0.02 us
  other arithmetic: 6.35 us -> 0 us
    all_gather x2 -> x0, waiting for transfers between devices: 286 us -> none  [the longest x1 143 us: shards(): weights = lax.all_gather(conv_kernel, 'lon', axis=2, tiled=True)]
    pallas_call x0 -> x1, Pallas kernels: none -> 84.2 us  [shards(): pl.pallas_call(kernel, out_shape=jax.ShapeDtypeStruct((4, 2, 16, 512), BF...]
    reduce_scatter x1 -> x0, waiting for transfers between devices: 43.6 us -> none  [shards(): lax.psum_scatter(local_fine.astype(jnp.bfloat16), 'ch', scatter_dimension...]
    ppermute x6 -> x0, starting transfers between devices: 34.6 us -> none  [the longest x3 26.3 us: padded_2(): lax.ppermute(lax.slice_in_dim(block, 0, width, axis=dim), axis, backward)]
    dot_general x25 -> x0, matrix products: 21.6 us -> none  [tap_dot(): jnp.einsum('rbjc,cn->rbjn', piece, weight, preferred_element_type=jnp.flo...]
    unnamed x42 -> x0, local copies, waits for them, and re-layouts: 18.6 us -> none
    slice x4 -> x0, local copies, waits for them, and re-layouts: 9.89 us -> none  [the longest x1 8.8 us: upsample(): term = tap_dot(piece, weights[a, c])]
    ppermute x6 -> x0, waiting for transfers between devices: 5.48 us -> none  [the longest x3 3.43 us: padded_2(): lax.ppermute(lax.slice_in_dim(block, 0, width, axis=dim), axis, backward)]
  transfers between devices with their start and end apart: 9 -> 0, of which waited for: 6 -> 0; matrix products, arithmetic and copies ran while one was open for 1% -> 0% of each run, Pallas kernels for 0% -> 0%
where the time goes in v1:
time: 86.2 us; the launch traced here: 86 us
  Pallas kernels  84.2 us (98%)
  local copies, waits for them, and re-layouts  1.79 us (2%)
    pallas_call x1, Pallas kernels, shards(): pl.pallas_call(kernel, out_shape=jax.ShapeDtypeStruct((4, 2, 16, 512), BF...  84.2 us

profile of v1, /device:TPU:1, one launch (start us, length us, event | category | flops | bytes accessed | tf_op | source)
XLA Modules:
  0.0 86.0 jit_solution(11388952343531667)
XLA Ops:
  0.0 84.2 %shard_map.55 = bf16[4,2,16,512]{3,2,1,0:T(8,128)(2,1)} custom-call(bf16[16,16,128]{2,1,0:T(8,128)(2,1)} %bitcast.12, bf16[16,8,128]{2,1,0:T(8,128)(2,1)} %bitcast.13, f32[1,512]{1,0:T(1,128)} %bitcast.14, bf16[9,8,512]{2,1,0:T(8,128)(2,1)} %bitcast.11, f32[1,512]{1,0:T(1,128)} %bitcast.15), custom_call_target="tpu_custom_call" | custom-call | tf_op jit(solution)/shard_map/pallas_call | solution.py:406
  84.2 0.9 %reshape.26 = bf16[4,2,4,4,512]{4,3,2,1,0:T(4,128)(2,1)S(1)} reshape(bf16[4,2,16,512]{3,2,1,0:T(8,128)(2,1)} %shard_map.55) | data formatting | bytes 262144 | tf_op jit(solution)/shard_map/reshape | solution.py:436
  85.2 0.1 copy.6
  85.3 0.7 reshape.27
